TPU v7x, 32 devices: a whole 2x2x4 slice. The times are simulated.
32 devices in a mesh: seq: 8 (over z, y), tp: 4 (over x, core).
Axes of the slice: x: 2, y: 2, z: 4, core: 2. Of those that a mesh axis runs over, the one named last changes fastest.
Arguments:
- tokens: bfloat16 [4, 2048, 1024], P('tp', 'seq'), may hold values from -6 to 6
- lengths: int32 [4], replicated, may hold values from 256 to 2048, as said below
- forget: float32 [8], replicated, as said below
- w_mix: bfloat16 [1024, 4096], replicated, may hold values from -0.1875 to 0.1875
- w_out: bfloat16 [1024, 1024], replicated, may hold values from -0.1875 to 0.1875
- w_gate: bfloat16 [1024, 2816], P(None, 'tp'), may hold values from -0.1875 to 0.1875
- w_up: bfloat16 [1024, 2816], P(None, 'tp'), may hold values from -0.1875 to 0.1875
- w_down: bfloat16 [1024, 2816], P(None, 'tp'), may hold values from -0.109375 to 0.109375
- cotangent: bfloat16 [4, 2048, 1024], P('tp', 'seq'), may hold values from -6 to 6
Outputs:
- out: bfloat16 [4, 2048, 1024], P('tp', 'seq')
- d_tokens: bfloat16 [4, 2048, 1024], P('tp', 'seq')
- d_mix: float32 [1024, 4096], P('seq')
- d_out: float32 [1024, 1024], P('seq')
- d_gate: float32 [1024, 2816], P('seq', 'tp')
- d_up: float32 [1024, 2816], P('seq', 'tp')
- d_down: float32 [1024, 2816], P('seq', 'tp')
Inputs may be any that keep to these rules, and one draw needn't show every extreme that they name: Positions at and after lengths[i] of sequence i are padding; in every draw one sequence has all 2048 positions. A head's state is multiplied by exp(-forget) for every position that it moves on.
All inputs are finite; a program needn't handle non-finite values.
Results may differ from a plain program's by a relative error of at most 0.02.
Values may be sent and summed in bfloat16 or wider, within the bound.
No kernel may reach another device: no remote copies, remote signals or barrier semaphores. Data moves between devices by JAX's collectives and lax.ppermute only.
A program may use at most 384 MiB of HBM per device.

v0:
```python
from functools import partial
import math

import jax
import jax.numpy as jnp
import numpy as np
from jax import lax
from jax.sharding import PartitionSpec as P

HEADS = 8
HEAD = 128


EPSILON = 1e-06


def entering(array, axis, join, neutral, backward):
    count = lax.axis_size(axis)
    place = lax.axis_index(axis)
    ahead = count - 1 - place if backward else place
    gathered = jax.tree.map(
        lambda a, kind: lax.all_gather(a.astype(kind), axis), array, (jnp.bfloat16, jnp.bfloat16)
    )
    state = jax.tree.map(lambda a, e: jnp.zeros_like(a) + jnp.asarray(e, a.dtype), array, neutral)

    def one(hop, state):
        source = count - 1 - hop if backward else hop
        return join(
            state,
            jax.tree.map(
                lambda a, own: lax.dynamic_index_in_dim(a, source, 0, False).astype(own.dtype),
                gathered,
                array,
            ),
        )

    return lax.fori_loop(0, ahead, one, state)


def simple_norm(value):
    return value * lax.rsqrt(jnp.mean(value * value, axis=-1, keepdims=True) + EPSILON)


def norm_back(value, upstream):
    return jax.vjp(simple_norm, value)[1](upstream)[0]


def contract(form, left, right):
    return jnp.einsum(
        form, left, right, precision=lax.Precision.HIGHEST, preferred_element_type=jnp.float32
    )


def product(form, left, right):
    return jnp.einsum(form, left, right, preferred_element_type=jnp.float32)


def rotation(places, width):
    table = np.floor(
        65536.0 / (2.0 * math.pi) * 10000.0 ** (-np.arange(width) / width) + 0.5
    ).astype(np.int32)
    phase = jnp.remainder(places[:, None] * jnp.asarray(table)[None, :], 65536)
    angle = phase.astype(jnp.float32) * (2.0 * math.pi / 65536.0)
    return (jnp.cos(angle), jnp.sin(angle))


def rotate_both(raw_query, raw_key, cosine, sine):

    def turn(values):
        values = jax.nn.silu(values)
        return jnp.concatenate([values * cosine[:, None, :], values * sine[:, None, :]], axis=-1)

    return (turn(raw_query), turn(raw_key))


def chain(earlier, later):
    return (earlier[0] * later[1][:, None, None] + later[0], earlier[1] * later[1])


def feed_forward(ffn_rows, gate_matrix, up_matrix, down_matrix):
    gate_pre = jnp.dot(ffn_rows, gate_matrix, preferred_element_type=jnp.float32)
    up_pre = jnp.dot(ffn_rows, up_matrix, preferred_element_type=jnp.float32)
    hidden = (gate_pre * up_pre).astype(jnp.bfloat16)
    down_terms = lax.dot_general(
        hidden, down_matrix, (((1,), (1,)), ((), ())), preferred_element_type=jnp.float32
    )
    return (gate_pre, up_pre, hidden, down_terms)


def feed_back(ffn_rows, down_grad, gate_pre, up_pre, hidden, gate_matrix, up_matrix, down_matrix):
    outer = (((0,), (0,)), ((), ()))
    inner = (((1,), (1,)), ((), ()))
    hidden_grad = jnp.dot(down_grad, down_matrix, preferred_element_type=jnp.float32)
    gate_grad = (hidden_grad * up_pre).astype(jnp.bfloat16)
    up_grad = (hidden_grad * gate_pre).astype(jnp.bfloat16)
    gate_weight_grad = lax.dot_general(
        ffn_rows, gate_grad, outer, preferred_element_type=jnp.float32
    )
    up_weight_grad = lax.dot_general(ffn_rows, up_grad, outer, preferred_element_type=jnp.float32)
    down_weight_grad = lax.dot_general(down_grad, hidden, outer, preferred_element_type=jnp.float32)
    rows_grad = lax.dot_general(gate_grad, gate_matrix, inner, preferred_element_type=jnp.float32)
    rows_grad = rows_grad + lax.dot_general(
        up_grad, up_matrix, inner, preferred_element_type=jnp.float32
    )
    return (rows_grad, gate_weight_grad, up_weight_grad, down_weight_grad)


def on_device(tokens, lengths, forget, w_mix, w_out, w_gate, w_up, w_down, cotangent):
    items, span, width = tokens.shape
    heads = HEADS
    head = HEAD
    rows = items * span
    outer = (((0,), (0,)), ((), ()))
    inner = (((1,), (1,)), ((), ()))
    place = lax.axis_index("seq")
    owner = lax.axis_index("tp")
    local_lengths = lax.dynamic_slice_in_dim(lengths, owner * items, items)
    ahead = jnp.arange(span, dtype=jnp.int32)
    places = place * span + ahead
    valid = (places[None, :] < local_lengths[:, None])[:, :, None]
    offsets = ahead.astype(jnp.float32)
    gap = ahead[:, None] - ahead[None, :]
    grid = jnp.where(
        gap[None] >= 0,
        jnp.exp(-forget[:, None, None] * jnp.maximum(gap, 0)[None].astype(jnp.float32)),
        0.0,
    )
    lead = jnp.exp(-forget[None, :] * (offsets + 1.0)[:, None])[None, :, :, None]
    tail = jnp.exp(-forget[None, :] * (span - 1.0 - offsets)[:, None])[None, :, :, None]
    first = jnp.exp(-forget[None, :] * offsets[:, None])[None, :, :, None]
    rear = jnp.exp(-forget[None, :] * (span - offsets)[:, None])[None, :, :, None]
    carried = jnp.exp(-forget * span)
    cosine, sine = rotation(places, head)
    inputs = tokens.astype(jnp.float32)
    normed_flat = simple_norm(inputs).astype(jnp.bfloat16).reshape(rows, width)
    projected = jnp.dot(normed_flat, w_mix, preferred_element_type=jnp.float32)
    raw_query = projected[:, :width].reshape(items, span, heads, head)
    raw_key = projected[:, width : 2 * width].reshape(items, span, heads, head)
    value_low = (
        projected[:, 2 * width : 3 * width].reshape(items, span, heads, head).astype(jnp.bfloat16)
    )
    update = projected[:, 3 * width :].reshape(items, span, width)
    rotated, turn_back = jax.vjp(partial(rotate_both, cosine=cosine, sine=sine), raw_query, raw_key)
    query_low = rotated[0].astype(jnp.bfloat16)
    key_low = rotated[1].astype(jnp.bfloat16)
    query = query_low.astype(jnp.float32)
    key = key_low.astype(jnp.float32)
    value = value_low.astype(jnp.float32)
    scores = (product("bthc,bshc->bhts", query_low, key_low) * grid[None]).astype(jnp.bfloat16)
    intra = product("bhts,bshe->bthe", scores, value_low)
    local_state = contract("bshc,bshe->bhce", key * tail, value)
    identity = (jnp.zeros_like(local_state), jnp.ones_like(carried))
    incoming = entering((local_state, carried), "seq", chain, identity, False)[0]
    inter = contract("bthc,bhce->bthe", query, incoming) * lead
    attention = (intra + inter).reshape(items, span, width)
    attention_normed = simple_norm(attention)
    gated_flat = (attention_normed * update).astype(jnp.bfloat16).reshape(rows, width)
    resid = inputs + jnp.dot(gated_flat, w_out, preferred_element_type=jnp.float32).reshape(
        items, span, width
    )
    ffn_in = simple_norm(resid).astype(jnp.bfloat16)
    grad_out = jnp.where(valid, cotangent.astype(jnp.float32), 0.0)
    down_low = grad_out.astype(jnp.bfloat16)
    gathered = lax.all_gather(ffn_in, "tp", axis=0, tiled=True)
    ffn_rows = gathered.reshape(-1, width)
    gate_pre, up_pre, hidden, down_terms = feed_forward(ffn_rows, w_gate, w_up, w_down)
    down = lax.psum_scatter(
        down_terms.reshape(-1, span, width).astype(jnp.bfloat16),
        "tp",
        scatter_dimension=0,
        tiled=True,
    ).astype(jnp.float32)
    down_grad = lax.all_gather(down_low, "tp", axis=0, tiled=True).reshape(-1, width)
    rows_grad, gate_weight_grad, up_weight_grad, down_weight_grad = feed_back(
        ffn_rows, down_grad, gate_pre, up_pre, hidden, w_gate, w_up, w_down
    )
    ffn_grad = lax.psum_scatter(
        rows_grad.reshape(-1, span, width).astype(jnp.bfloat16),
        "tp",
        scatter_dimension=0,
        tiled=True,
    ).astype(jnp.float32)
    out = jnp.where(valid, resid + down, 0.0).astype(jnp.bfloat16)
    resid_grad = grad_out + norm_back(resid, ffn_grad)
    mix_grad = resid_grad.astype(jnp.bfloat16).reshape(rows, width)
    out_weight_grad = lax.dot_general(
        gated_flat, mix_grad, outer, preferred_element_type=jnp.float32
    )
    gated_grad = lax.dot_general(
        mix_grad, w_out, inner, preferred_element_type=jnp.float32
    ).reshape(items, span, width)
    update_grad = gated_grad * attention_normed
    grad_low = (
        norm_back(attention, gated_grad * update)
        .reshape(items, span, heads, head)
        .astype(jnp.bfloat16)
    )
    attention_grad = grad_low.astype(jnp.float32)
    moment = contract("bthc,bthe->bhce", query * first, attention_grad)
    after = entering((moment, carried), "seq", chain, identity, True)[0]
    score_grad = (product("bthe,bshe->bhts", grad_low, value_low) * grid[None]).astype(jnp.bfloat16)
    query_grad = (
        product("bhts,bshc->bthc", score_grad, key_low)
        + contract("bthe,bhce->bthc", attention_grad, incoming) * lead
    )
    key_grad = (
        product("bhts,bthc->bshc", score_grad, query_low)
        + contract("bshe,bhce->bshc", value, after) * rear
    )
    value_grad = (
        product("bhts,bthe->bshe", scores, grad_low)
        + contract("bshc,bhce->bshe", key, after) * rear
    )
    raw_query_grad, raw_key_grad = turn_back((query_grad, key_grad))
    projected_grad = jnp.concatenate(
        [
            raw_query_grad.reshape(rows, width),
            raw_key_grad.reshape(rows, width),
            value_grad.reshape(rows, width),
            update_grad.reshape(rows, width),
        ],
        axis=1,
    ).astype(jnp.bfloat16)
    mix_weight_grad = lax.dot_general(
        normed_flat, projected_grad, outer, preferred_element_type=jnp.float32
    )
    normed_grad = lax.dot_general(projected_grad, w_mix, inner, preferred_element_type=jnp.float32)
    d_tokens = (resid_grad + norm_back(inputs, normed_grad.reshape(items, span, width))).astype(
        jnp.bfloat16
    )
    summed = (
        lax.psum_scatter(mix_weight_grad, "seq", scatter_dimension=0, tiled=True),
        lax.psum_scatter(out_weight_grad, "seq", scatter_dimension=0, tiled=True),
        lax.psum_scatter(gate_weight_grad, "seq", scatter_dimension=0, tiled=True),
        lax.psum_scatter(up_weight_grad, "seq", scatter_dimension=0, tiled=True),
        lax.psum_scatter(down_weight_grad, "seq", scatter_dimension=0, tiled=True),
    )
    gate_sum, up_sum, down_sum = (summed[2], summed[3], summed[4])
    mix_sum, out_sum = (
        lax.psum(summed[0].astype(jnp.bfloat16), "tp").astype(jnp.float32),
        lax.psum(summed[1].astype(jnp.bfloat16), "tp").astype(jnp.float32),
    )
    return (out, d_tokens, mix_sum, out_sum, gate_sum, up_sum, down_sum)


def solution(mesh):
    in_specs = (
        P("tp", "seq", None),
        P(),
        P(),
        P(),
        P(),
        P(None, "tp"),
        P(None, "tp"),
        P(None, "tp"),
        P("tp", "seq", None),
    )
    out_specs = (
        P("tp", "seq", None),
        P("tp", "seq", None),
        P("seq", None),
        P("seq", None),
        P("seq", "tp"),
        P("seq", "tp"),
        P("seq", "tp"),
    )
    return jax.shard_map(
        on_device, mesh=mesh, in_specs=in_specs, out_specs=out_specs, check_vma=False
    )
```

profile of v0, /device:TPU:0, one launch (start us, length us, event | category | flops | bytes accessed | tf_op | source)
XLA Modules:
  0.0 982.6 jit_solution(16597565705403237700)
XLA Ops:
  9.3 6.0 fusion.68
  15.3 2.1 fusion.85
  18.1 1.9 multiply_convert_fusion.9
  20.0 3.0 fusion.13
  24.6 23.5 %all-reduce = bf16[64]{0:T(256)(128)(2,1)S(1)} all-reduce(bf16[64]{0:T(256)(128)(2,1)S(1)} %dynamic-update-slice), channel_id=2, replica_groups=mesh['seq'=8,'tp'=4] {'seq'}, use_global_device_ids=true, to_apply=%add | all-reduce | flops 64 | bytes 256
  48.2 1.9 multiply_convert_fusion.4
  51.2 2.7 convolution_bitcast_fusion.4
  53.9 45.6 %all-gather.12.cloned.1.call-done = bf16[64,256,128]{2,1,0:T(8,128)(2,1)} async-done(((bf16[8,256,128]{2,1,0:T(8,128)(2,1)}), bf16[64,256,128]{2,1,0:T(8,128)(2,1)}) %all-gather.12.cloned.1.call-update) | async-done | bytes 4194320 | tf_op jit(solution)/shard_map/all_gather | solution.py:22
  99.5 3.5 multiply_reduce_fusion.2
  103.1 2.6 copy.83
  111.5 2.0 fusion.46
  113.7 27.0 %all-gather.8.cloned.1.call-done = bf16[4,256,1024]{2,1,0:T(8,128)(2,1)} async-done(((bf16[1,256,1024]{2,1,0:T(8,128)(2,1)}), bf16[4,256,1024]{2,1,0:T(8,128)(2,1)}) %all-gather.8.cloned.1.call-update) | async-done | bytes 2097168 | tf_op jit(solution)/shard_map/all_gather | solution.py:164
  140.8 5.5 fusion.87
  146.3 3.2 fusion.86
  149.5 16.0 %all-gather.10.cloned.1.call-done = bf16[4,256,1024]{2,1,0:T(8,128)(2,1)} async-done(((bf16[1,256,1024]{2,1,0:T(8,128)(2,1)}), bf16[4,256,1024]{2,1,0:T(8,128)(2,1)}) %all-gather.10.cloned.1.call-update) | async-done | bytes 2097168 | tf_op jit(solution)/shard_map/all_gather | solution.py:173
  165.5 6.8 multiply_convert_fusion
  172.3 1.8 fusion.88
  174.7 3.2 add_convert_fusion
  177.9 5.0 convolution_convert_fusion
  183.2 26.2 %reduce-scatter.10.cloned.1.call-done = bf16[1,256,1024]{2,1,0:T(8,128)(2,1)} async-done(((bf16[4,256,1024]{2,1,0:T(8,128)(2,1)}), bf16[1,256,1024]{2,1,0:T(8,128)(2,1)}) %reduce-scatter.10.cloned.1.call-update) | async-done | bytes 524304 | tf_op jit(solution)/shard_map/reduce_scatter | solution.py:177
  211.0 32.4 %reduce-scatter.8.cloned.1.call-done = bf16[1,256,1024]{2,1,0:T(8,128)(2,1)} async-done(((bf16[4,256,1024]{2,1,0:T(8,128)(2,1)}), bf16[1,256,1024]{2,1,0:T(8,128)(2,1)}) %reduce-scatter.8.cloned.1.call-update) | async-done | bytes 524304 | tf_op jit(solution)/shard_map/reduce_scatter | solution.py:167
  243.4 3.1 fusion.20
  246.5 2.5 multiply_reduce_fusion
  250.4 2.2 copy.89
  252.6 4.0 fusion.16
  256.7 3.8 fusion.54
  260.8 2.6 copy.87
  263.4 2.6 copy.88
  266.0 2.5 convolution_bitcast_fusion.3
  268.5 1.9 multiply_convert_fusion.3
  273.4 2.4 fusion.1
  275.8 54.5 %all-gather.14.cloned.1.call-done = bf16[64,256,128]{2,1,0:T(8,128)(2,1)} async-done(((bf16[8,256,128]{2,1,0:T(8,128)(2,1)}), bf16[64,256,128]{2,1,0:T(8,128)(2,1)}) %all-gather.14.cloned.1.call-update) | async-done | bytes 4194320 | tf_op jit(solution)/shard_map/all_gather | solution.py:22
  330.3 14.3 %while.27 = (s32[]{:T(128)}, f32[1,8,256,128]{3,2,1,0:T(8,128)S(1)}, s32[]{:T(128)}, bf16[8,8]{1,0:T(8,128)(2,1)}, bf16[8,1,8,256,128]{4,3,2,1,0:T(8,128)(2,1)},...) while((s32[]{:T(128)}, f32[1,8,256,128]{3,2,1,0:T(8,128)S(1)}, s32[]{:T(128)}, bf16[8,8]{1,0:T(8,128)(2,1)}, ...), condition=%wide.region_10.11_spmd, body=%wide.region_9.10_spmd.sunk | while | flops 786446 | bytes 2621675 | solution.py:37
  344.7 2.0 fusion.12
  348.0 3.1 fusion
  354.7 8.4 fusion.58
  363.1 56.9 %reduce-scatter.14.cloned.1.call-done = f32[128,1024]{1,0:T(8,128)} async-done(((f32[1024,1024]{1,0:T(8,128)}), f32[128,1024]{1,0:T(8,128)}) %reduce-scatter.14.cloned.1.call-update) | async-done | bytes 524304 | tf_op jit(solution)/shard_map/reduce_scatter | solution.py:233
  421.8 284.8 %reduce-scatter.12.cloned.1.call-done = f32[128,4096]{1,0:T(8,128)} async-done(((f32[1024,4096]{1,0:T(8,128)}), f32[128,4096]{1,0:T(8,128)}) %reduce-scatter.12.cloned.1.call-update) | async-done | bytes 2097168 | tf_op jit(solution)/shard_map/reduce_scatter | solution.py:232
  706.6 2.7 convert_element_type.269
  709.4 4.6 fusion.91
  715.4 4.9 fusion.90
  721.6 4.9 fusion.89
  727.9 5.9 fusion.32
  734.9 13.0 %all-reduce.4.cloned.1.call-done = (bf16[128,4096]{1,0:T(8,128)(2,1)}, bf16[128,1024]{1,0:T(8,128)(2,1)}) async-done(((bf16[128,4096]{1,0:T(8,128)(2,1)}, bf16[128,1024]{1,0:T(8,128)(2,1)}), (bf16[128,4096]{1,0:T(8,128)(2,1)}, bf16[128,1024]{1,0:T(8,128)(2,1)})) %all-reduce.4.cloned.1.call-update) | async-done | bytes 1310736 | tf_op jit(solution)/shard_map/psum | solution.py:240
  749.7 2.8 convert_element_type.270
  752.5 71.8 %reduce-scatter.20.cloned.1.call-done = f32[128,704]{0,1:T(8,128)} async-done(((f32[1024,704]{0,1:T(8,128)}), f32[128,704]{0,1:T(8,128)}) %reduce-scatter.20.cloned.1.call-update) | async-done | bytes 360464 | tf_op jit(solution)/shard_map/reduce_scatter | solution.py:236
  824.2 75.6 %reduce-scatter.18.cloned.1.call-done = f32[128,704]{0,1:T(8,128)} async-done(((f32[1024,704]{0,1:T(8,128)}), f32[128,704]{0,1:T(8,128)}) %reduce-scatter.18.cloned.1.call-update) | async-done | bytes 360464 | tf_op jit(solution)/shard_map/reduce_scatter | solution.py:235
  899.8 75.4 %reduce-scatter.16.cloned.1.call-done = f32[128,704]{0,1:T(8,128)} async-done(((f32[1024,704]{0,1:T(8,128)}), f32[128,704]{0,1:T(8,128)}) %reduce-scatter.16.cloned.1.call-update) | async-done | bytes 360464 | tf_op jit(solution)/shard_map/reduce_scatter | solution.py:234
  (187 shorter events, 45.5 us)
Async XLA Ops:
  7.2 100.2 %copy-start = (bf16[1024,1024]{1,0:T(8,128)(2,1)S(1)}, bf16[1024,1024]{1,0:T(8,128)(2,1)}, u32[]{:S(2)}) copy-start(bf16[1024,1024]{1,0:T(8,128)(2,1)} %param.18) | copy-start | bytes 6291460
  7.2 92.2 %all-gather.12.cloned.1.call-start = ((), (), s32[]{:S(2)}) async-start(), calls=%async_computation.16 | async-start | bytes 4718592 | tf_op jit(solution)/shard_map/all_gather | solution.py:22
  9.3 38.9 %copy-start.45 = (f32[8]{0:T(128)}, f32[8]{0:T(128)S(1)}, u32[]{:S(2)}) copy-start(f32[8]{0:T(128)S(1)} %get-tuple-element.205) | copy-start | bytes 100
  15.3 4.7 copy-start.2
  15.3 2.1 copy-start.47
  19.9 28.3 %copy-start.13 = (bf16[256,8,128]{2,0,1:T(8,128)(2,1)}, bf16[256,8,128]{2,0,1:T(8,128)(2,1)S(1)}, u32[]{:S(2)}) copy-start(bf16[256,8,128]{2,0,1:T(8,128)(2,1)S(1)} %get-tuple-element.192) | copy-start | bytes 1572868
  19.9 28.3 %copy-start.16 = (bf16[256,8,128]{2,0,1:T(8,128)(2,1)}, bf16[256,8,128]{2,0,1:T(8,128)(2,1)S(1)}, u32[]{:S(2)}) copy-start(bf16[256,8,128]{2,0,1:T(8,128)(2,1)S(1)} %get-tuple-element.193) | copy-start | bytes 1572868
  19.9 3.1 copy-start.53
  20.0 79.5 %copy-start.40 = (f32[256,8]{0,1:T(8,128)}, f32[256,8]{0,1:T(8,128)S(1)}, u32[]{:S(2)}) copy-start(f32[256,8]{0,1:T(8,128)S(1)} %get-tuple-element.203) | copy-start | bytes 24580
  23.0 117.7 %all-gather.8.cloned.1.call-start = ((), (), s32[]{:S(2)}) async-start(), calls=%async_computation.7 | async-start | bytes 2621440 | tf_op jit(solution)/shard_map/all_gather | solution.py:164
  48.2 2.0 copy-start.42
  48.2 2.0 copy-start.38
  99.5 3.5 copy-start.44
  110.2 55.3 %all-gather.10.cloned.1.call-start = ((), (), s32[]{:S(2)}) async-start(), calls=%async_computation.9 | async-start | bytes 2621440 | tf_op jit(solution)/shard_map/all_gather | solution.py:173
  113.5 95.9 %reduce-scatter.10.cloned.1.call-start = ((), (), s32[]{:S(2)}) async-start(), calls=%async_computation.10 | async-start | bytes 2621440 | tf_op jit(solution)/shard_map/reduce_scatter | solution.py:177
  140.7 5.5 copy-start.48
  140.7 5.5 copy-start.49
  165.5 6.8 copy-start.50
  172.3 2.4 copy-start.51
  177.9 65.5 %reduce-scatter.8.cloned.1.call-start = ((), (), s32[]{:S(2)}) async-start(), calls=%async_computation.8 | async-start | bytes 2621440 | tf_op jit(solution)/shard_map/reduce_scatter | solution.py:167
  183.0 147.2 %all-gather.14.cloned.1.call-start = ((), (), s32[]{:S(2)}) async-start(), calls=%async_computation.17 | async-start | bytes 4718592 | tf_op jit(solution)/shard_map/all_gather | solution.py:22
  243.4 3.1 copy-start.3
  246.5 2.5 copy-start.6
  246.5 2.6 copy-start.5
  249.1 3.5 copy-start.19
  249.1 3.5 copy-start.20
  250.4 6.2 copy-start.7
  256.6 163.4 %reduce-scatter.14.cloned.1.call-start = ((), (), s32[]{:S(2)}) async-start(), calls=%async_computation.12 | async-start | bytes 4718592 | tf_op jit(solution)/shard_map/reduce_scatter | solution.py:233
  260.5 446.1 %reduce-scatter.12.cloned.1.call-start = ((), (), s32[]{:S(2)}) async-start(), calls=%async_computation.11 | async-start | bytes 18874368 | tf_op jit(solution)/shard_map/reduce_scatter | solution.py:232
  260.7 5.3 copy-start.22
  263.4 5.2 copy-start.39
  263.4 5.2 copy-start.43
  263.4 5.2 copy-start.46
  330.3 14.4 %copy-start.15 = (bf16[256,8,128]{2,0,1:T(8,128)(2,1)S(1)}, bf16[256,8,128]{2,0,1:T(8,128)(2,1)}, u32[]{:S(2)}) copy-start(bf16[256,8,128]{2,0,1:T(8,128)(2,1)} %copy-done.13) | copy-start | bytes 1572868
  330.3 14.4 %copy-start.18 = (bf16[256,8,128]{2,0,1:T(8,128)(2,1)S(1)}, bf16[256,8,128]{2,0,1:T(8,128)(2,1)}, u32[]{:S(2)}) copy-start(bf16[256,8,128]{2,0,1:T(8,128)(2,1)} %copy-done.16) | copy-start | bytes 1572868
  330.3 14.4 %copy-start.29 = (f32[1,256,8,128]{1,3,2,0:T(8,128)S(1)}, f32[1,256,8,128]{1,3,2,0:T(8,128)}, u32[]{:S(2)}) copy-start(f32[1,256,8,128]{1,3,2,0:T(8,128)} %convolution_bitcast_fusion.3) | copy-start | bytes 3145732
  347.9 3.2 copy-start.11
  348.0 3.2 copy-start.30
  348.0 3.2 copy-start.31
  353.1 10.0 %copy-start.32 = (bf16[256,1024]{1,0:T(8,128)(2,1)}, bf16[256,1024]{1,0:T(8,128)(2,1)S(1)}, u32[]{:S(2)}) copy-start(bf16[256,1024]{1,0:T(8,128)(2,1)S(1)} %copy.84) | copy-start | bytes 1572868
  354.6 8.4 copy-start.34
  363.1 384.9 %all-reduce.4.cloned.1.call-start = ((), (), s32[]{:S(2)}) async-start(), calls=%async_computation.18 | async-start | bytes 2621440 | tf_op jit(solution)/shard_map/psum | solution.py:240
  421.8 287.6 %copy-start.12 = (bf16[4,256,1024]{2,1,0:T(8,128)(2,1)S(1)}, bf16[4,256,1024]{2,1,0:T(8,128)(2,1)}, u32[]{:S(2)}) copy-start(bf16[4,256,1024]{2,1,0:T(8,128)(2,1)} %all-gather.10.cloned.1.call-done) | copy-start | bytes 6291460
  709.3 114.9 %reduce-scatter.20.cloned.1.call-start = ((), (), s32[]{:S(2)}) async-start(), calls=%async_computation.15 | async-start | bytes 3244032 | tf_op jit(solution)/shard_map/reduce_scatter | solution.py:236
  714.0 185.8 %reduce-scatter.18.cloned.1.call-start = ((), (), s32[]{:S(2)}) async-start(), calls=%async_computation.14 | async-start | bytes 3244032 | tf_op jit(solution)/shard_map/reduce_scatter | solution.py:235
  720.2 255.0 %reduce-scatter.16.cloned.1.call-start = ((), (), s32[]{:S(2)}) async-start(), calls=%async_computation.13 | async-start | bytes 3244032 | tf_op jit(solution)/shard_map/reduce_scatter | solution.py:234
  727.9 5.9 copy-start.8
  733.8 241.4 %copy-start.1 = (bf16[1024,1024]{1,0:T(8,128)(2,1)S(1)}, bf16[1024,1024]{1,0:T(8,128)(2,1)}, u32[]{:S(2)}) copy-start(bf16[1024,1024]{1,0:T(8,128)(2,1)} %param.18) | copy-start | bytes 6291460
  (18 other events, 26.1 us)
Sparse Core Ops, SparseCore 0:
  23.1 76.2 all-gather.11
  110.3 30.3 all-gather.7
  142.9 22.5 all-gather.9
  178.0 31.3 reduce-scatter.9
  212.0 31.3 reduce-scatter.7
  256.7 73.4 all-gather.13
  333.8 86.1 reduce-scatter.13
  424.3 282.3 reduce-scatter.11
  709.7 38.1 all-reduce.3
  751.9 72.2 reduce-scatter.19
  828.4 71.3 reduce-scatter.17
  903.8 71.3 reduce-scatter.15
where the time goes:
time: 992 us; the launch traced here: 983 us
  waiting for transfers between devices  779 us (79%)
  matrix products  96.6 us (10%)
  other arithmetic  41.7 us (4%)
  local copies, waits for them, and re-layouts  23.8 us (2%)
  blocking collectives  23.5 us (2%)
  between operations  16 us (2%)
    reduce_scatter x1, waiting for transfers between devices, on_device(): lax.psum_scatter(mix_weight_grad, 'seq', scatter_dimension=0, tiled=True)  285 us
    all_gather x2, waiting for transfers between devices, entering(): lax.all_gather(a.astype(kind), axis)  100 us
    reduce_scatter x1, waiting for transfers between devices, on_device(): lax.psum_scatter(up_weight_grad, 'seq', scatter_dimension=0, tiled=True)  75.6 us
    reduce_scatter x1, waiting for transfers between devices, on_device(): lax.psum_scatter(gate_weight_grad, 'seq', scatter_dimension=0, tiled=True)  75.4 us
    reduce_scatter x1, waiting for transfers between devices, on_device(): lax.psum_scatter(down_weight_grad, 'seq', scatter_dimension=0, tiled=True)  71.8 us
    reduce_scatter x1, waiting for transfers between devices, on_device(): lax.psum_scatter(out_weight_grad, 'seq', scatter_dimension=0, tiled=True)  56.9 us
    reduce_scatter x1, waiting for transfers between devices, on_device(): lax.psum_scatter(down_terms.reshape(-1, span, width).astype(jnp.bfloat16)...  32.4 us
    all_gather x1, waiting for transfers between devices, on_device(): gathered = lax.all_gather(ffn_in, 'tp', axis=0, tiled=True)  27 us
  transfers between devices with their start and end apart: 12, of which 12 were waited for; matrix products, arithmetic and copies ran while one was open for 10% of the time, Pallas kernels for 0%

commit v1 on v0

v1 whole, which is shorter than its diff:
```python
from functools import partial
import math

import jax
import jax.numpy as jnp
import numpy as np
from jax import lax
from jax.sharding import PartitionSpec as P

HEADS = 8
HEAD = 128
EPSILON = 1e-06
BF = jnp.bfloat16
F32 = jnp.float32


def simple_norm(value):
    return value * lax.rsqrt(jnp.mean(value * value, axis=-1, keepdims=True) + EPSILON)


def norm_back(value, upstream):
    r = lax.rsqrt(jnp.mean(value * value, axis=-1, keepdims=True) + EPSILON)
    return r * upstream - value * (r * r * r * jnp.mean(value * upstream, axis=-1, keepdims=True))


def product(form, left, right):
    return jnp.einsum(form, left, right, preferred_element_type=F32)


def dot_tn(left, right, kind=BF):
    return lax.dot_general(left, right, (((0,), (0,)), ((), ())), preferred_element_type=F32).astype(kind)


def dot_nt(left, right):
    return lax.dot_general(left, right, (((1,), (1,)), ((), ())), preferred_element_type=F32)


def rotation(places, width):
    table = np.floor(
        65536.0 / (2.0 * math.pi) * 10000.0 ** (-np.arange(width) / width) + 0.5
    ).astype(np.int32)
    phase = jnp.remainder(places[:, None] * jnp.asarray(table)[None, :], 65536)
    angle = phase.astype(F32) * (2.0 * math.pi / 65536.0)
    return (jnp.cos(angle), jnp.sin(angle))


def swap(array, axis, bit):
    count = lax.axis_size(axis)
    return lax.ppermute(array, axis, [(i, i ^ bit) for i in range(count)])


def shift(array, axis, hop):
    count = lax.axis_size(axis)
    pairs = [(i, i + hop) for i in range(count) if 0 <= i + hop < count]
    return lax.ppermute(array, axis, pairs)


def gather_tp(array):
    near = swap(array, "tp", 1)
    far = swap(array, "tp", 2)
    return [array, near, far, swap(far, "tp", 1)]


def scatter_tp(parts):
    p0, p1, p2, p3 = parts
    r1, r3 = swap(jnp.stack([p1, p3]), "tp", 1)
    far = swap((p2.astype(F32) + r3.astype(F32)).astype(BF), "tp", 2)
    return p0.astype(F32) + r1.astype(F32) + far.astype(F32)


def exchange_tp(pieces, owner):
    mine = lax.dynamic_index_in_dim(pieces, owner, 0, False)
    out = [mine]
    for bit in (1, 2, 3):
        out.append(swap(lax.dynamic_index_in_dim(pieces, owner ^ bit, 0, False), "tp", bit))
    return out


def collect_tp(array, owner):
    parts = gather_tp(array)
    return [lax.select_n(owner, *[parts[j ^ k] for k in range(4)]) for j in range(4)]


def reduce_seq(array):
    count = lax.axis_size("seq")
    if count != 8:
        return lax.psum_scatter(array, "seq", scatter_dimension=0, tiled=True).astype(F32)
    place = lax.axis_index("seq")
    side = place % 2
    layer = place // 2
    rows, columns = array.shape
    blocks = array.reshape(count // 2, 2, rows // count, columns)
    keep = lax.dynamic_index_in_dim(blocks, side, 1, False)
    send = lax.dynamic_index_in_dim(blocks, 1 - side, 1, False)
    total = keep.astype(F32) + swap(send, "seq", 1).astype(F32)
    low = total.astype(BF)
    result = lax.dynamic_index_in_dim(total, layer, 0, False)
    for bit in (1, 2, 3):
        part = lax.dynamic_index_in_dim(low, layer ^ bit, 0, False)
        result = result + swap(part, "seq", 2 * bit).astype(F32)
    return result


def entering_any(state, carried, backward):
    count = lax.axis_size("seq")
    place = lax.axis_index("seq")
    ahead = count - 1 - place if backward else place
    gathered = lax.all_gather(state.astype(BF), "seq")

    def one(hop, total):
        source = count - 1 - hop if backward else hop
        part = lax.dynamic_index_in_dim(gathered, source, 0, False).astype(F32)
        return total * carried[:, None, None] + part

    return lax.fori_loop(0, ahead, one, jnp.zeros(state.shape, F32)).astype(BF)


def entering(state, carried, backward):
    count = lax.axis_size("seq")
    if count != 8:
        return entering_any(state, carried, backward)
    place = lax.axis_index("seq")
    side = place % 2
    half = HEADS // 2
    first = side == (1 if backward else 0)
    hop = -2 if backward else 2
    low = state.astype(BF)
    keep = lax.dynamic_slice_in_dim(low, side * half, half).astype(F32)
    send = lax.dynamic_slice_in_dim(low, (1 - side) * half, half)
    other = swap(send, "seq", 1).astype(F32)
    rate = lax.dynamic_slice_in_dim(carried, side * half, half)[:, None, None]
    pair = jnp.where(first, keep * rate + other, other * rate + keep)
    near = shift(pair.astype(BF), "seq", hop).astype(F32)
    far = shift((pair + rate * rate * near).astype(BF), "seq", 2 * hop).astype(F32)
    before = near + rate * rate * far
    mine = jnp.where(first, before, before * rate + other).astype(BF)
    theirs = swap(jnp.where(first, before * rate + keep, before).astype(BF), "seq", 1)
    return jnp.where(side == 0, jnp.concatenate([mine, theirs]), jnp.concatenate([theirs, mine]))


def on_device(tokens, lengths, forget, w_mix, w_out, w_gate, w_up, w_down, cotangent):
    items, span, width = tokens.shape
    heads = HEADS
    head = HEAD
    place = lax.axis_index("seq")
    owner = lax.axis_index("tp")
    length = lax.dynamic_index_in_dim(lengths, owner, 0, False)
    ahead = jnp.arange(span, dtype=jnp.int32)
    places = place * span + ahead
    valid = (places < length)[:, None]
    offsets = ahead.astype(F32)
    gap = ahead[:, None] - ahead[None, :]
    grid = jnp.where(
        gap[None] >= 0,
        jnp.exp(-forget[:, None, None] * jnp.maximum(gap, 0)[None].astype(F32)),
        0.0,
    )
    lead = jnp.exp(-forget[None, :] * (offsets + 1.0)[:, None])[:, :, None]
    tail = jnp.exp(-forget[None, :] * (span - 1.0 - offsets)[:, None])[:, :, None]
    first = jnp.exp(-forget[None, :] * offsets[:, None])[:, :, None]
    rear = jnp.exp(-forget[None, :] * (span - offsets)[:, None])[:, :, None]
    carried = jnp.exp(-forget * span)
    cosine, sine = rotation(places, head)
    cosine, sine = cosine[:, None, :], sine[:, None, :]
    inputs = tokens.reshape(span, width).astype(F32)
    normed = simple_norm(inputs).astype(BF)

    def turn(values):
        values = jax.nn.silu(values)
        return jnp.concatenate([values * cosine, values * sine], axis=-1).astype(BF)

    def turn_back(raw, grad):
        gate = jax.nn.sigmoid(raw)
        slope = gate * (1.0 + raw * (1.0 - gate))
        return (slope * (grad[:, :, :head] * cosine + grad[:, :, head:] * sine)).reshape(span, width)

    key_value = jnp.dot(normed, w_mix[:, width : 3 * width], preferred_element_type=F32)
    raw_key = key_value[:, :width].reshape(span, heads, head)
    value = key_value[:, width:].reshape(span, heads, head).astype(BF)
    key = turn(raw_key)
    local_state = product("bhc,bhe->hce", key, (value * tail).astype(BF))
    incoming = entering(local_state, carried, False)

    raw_query = jnp.dot(normed, w_mix[:, :width], preferred_element_type=F32).reshape(span, heads, head)
    update = jnp.dot(normed, w_mix[:, 3 * width :], preferred_element_type=F32)
    query = turn(raw_query)
    scores = (product("thc,shc->hts", query, key) * grid).astype(BF)
    intra = product("hts,she->the", scores, value)
    grad_out = jnp.where(valid, cotangent.reshape(span, width).astype(F32), 0.0)
    down_grad = jnp.concatenate(gather_tp(grad_out.astype(BF)))
    hidden_grad = jnp.dot(down_grad, w_down, preferred_element_type=F32)
    normed_all = jnp.concatenate(gather_tp(normed))

    inter = product("thc,hce->the", query, incoming) * lead
    attention = (intra + inter).reshape(span, width)
    attention_normed = simple_norm(attention)
    gated = (attention_normed * update).astype(BF)
    resid = inputs + jnp.dot(gated, w_out, preferred_element_type=F32)
    ffn_in = simple_norm(resid).astype(BF)
    ffn_rows = jnp.concatenate(gather_tp(ffn_in))
    gated_all = jnp.concatenate(gather_tp(gated))

    gate_pre = jnp.dot(ffn_rows, w_gate, preferred_element_type=F32)
    up_pre = jnp.dot(ffn_rows, w_up, preferred_element_type=F32)
    hidden = (gate_pre * up_pre).astype(BF)
    gate_grad = (hidden_grad * up_pre).astype(BF)
    up_grad = (hidden_grad * gate_pre).astype(BF)
    rows_grad = (dot_nt(gate_grad, w_gate) + dot_nt(up_grad, w_up)).astype(BF)
    ffn_grad = scatter_tp(list(rows_grad.reshape(4, span, width)))
    down_terms = dot_nt(hidden, w_down).astype(BF)
    down = scatter_tp(list(down_terms.reshape(4, span, width)))
    out = jnp.where(valid, resid + down, 0.0).astype(BF)

    resid_grad = grad_out + norm_back(resid, ffn_grad)
    mix_grad = resid_grad.astype(BF)
    gated_grad = dot_nt(mix_grad, w_out)
    update_grad = gated_grad * attention_normed
    attention_grad = norm_back(attention, gated_grad * update).reshape(span, heads, head).astype(BF)
    moment = product("bhc,bhe->hce", query, (attention_grad * first).astype(BF))
    after = entering(moment, carried, True)

    score_grad = (product("the,she->hts", attention_grad, value) * grid).astype(BF)
    query_grad = (
        product("hts,shc->thc", score_grad, key) + product("the,hce->thc", attention_grad, incoming) * lead
    )
    early = jnp.concatenate([turn_back(raw_query, query_grad), update_grad], axis=1).astype(BF)
    quarter = width // 4
    early_pieces = jnp.stack(
        [
            jnp.concatenate(
                [block[:, j * quarter : (j + 1) * quarter] for block in (early[:, :width], early[:, width:], mix_grad)],
                axis=1,
            )
            for j in range(4)
        ]
    )
    early_all = jnp.concatenate(exchange_tp(early_pieces, owner))
    early_part = jnp.concatenate(
        [dot_tn(normed_all, early_all[:, : 2 * quarter]), dot_tn(gated_all, early_all[:, 2 * quarter :])], axis=1
    )
    early_sum = reduce_seq(early_part)

    gate_weight = dot_tn(ffn_rows, gate_grad)
    up_weight = dot_tn(ffn_rows, up_grad)
    down_weight = dot_tn(down_grad, hidden)

    def over_seq(array):
        return lax.psum_scatter(array, "seq", scatter_dimension=0, tiled=True).astype(F32)

    gate_sum, up_sum, down_sum = over_seq(gate_weight), over_seq(up_weight), over_seq(down_weight)

    key_grad = product("hts,thc->shc", score_grad, query) + product("she,hce->shc", value, after) * rear
    value_grad = product("hts,the->she", scores, attention_grad) + product("shc,hce->she", key, after) * rear
    late = jnp.concatenate([turn_back(raw_key, key_grad), value_grad.reshape(span, width)], axis=1).astype(BF)
    late_pieces = jnp.stack(
        [
            jnp.concatenate(
                [block[:, j * quarter : (j + 1) * quarter] for block in (late[:, :width], late[:, width:])], axis=1
            )
            for j in range(4)
        ]
    )
    late_all = jnp.concatenate(exchange_tp(late_pieces, owner))
    late_sum = reduce_seq(dot_tn(normed_all, late_all))

    projected_grad = jnp.concatenate([early[:, :width], late, early[:, width:]], axis=1)
    normed_grad = dot_nt(projected_grad, w_mix)
    d_tokens = (resid_grad + norm_back(inputs, normed_grad)).astype(BF)

    early_full = collect_tp(early_sum.astype(BF), owner)
    late_full = collect_tp(late_sum.astype(BF), owner)
    mix_sum = jnp.concatenate(
        [p[:, :quarter] for p in early_full]
        + [p[:, :quarter] for p in late_full]
        + [p[:, quarter:] for p in late_full]
        + [p[:, quarter : 2 * quarter] for p in early_full],
        axis=1,
    ).astype(F32)
    out_sum = jnp.concatenate([p[:, 2 * quarter :] for p in early_full], axis=1).astype(F32)
    shape = (items, span, width)
    return (out.reshape(shape), d_tokens.reshape(shape), mix_sum, out_sum, gate_sum, up_sum, down_sum)


def solution(mesh):
    in_specs = (
        P("tp", "seq", None),
        P(),
        P(),
        P(),
        P(),
        P(None, "tp"),
        P(None, "tp"),
        P(None, "tp"),
        P("tp", "seq", None),
    )
    out_specs = (
        P("tp", "seq", None),
        P("tp", "seq", None),
        P("seq", None),
        P("seq", None),
        P("seq", "tp"),
        P("seq", "tp"),
        P("seq", "tp"),
    )
    return jax.shard_map(
        on_device, mesh=mesh, in_specs=in_specs, out_specs=out_specs, check_vma=False
    )
```

time: 992 us -> 384 us (0.39)
  waiting for transfers between devices: 779 us -> 150 us
  starting transfers between devices: 1.18 us -> 52.9 us
  local copies, waits for them, and re-layouts: 23.8 us -> 52.6 us
  matrix products: 96.6 us -> 71.1 us
  blocking collectives: 23.5 us -> 0 us
    reduce_scatter x7 -> x0, waiting for transfers between devices: 623 us -> none  [the longest x1 285 us: on_device(): lax.psum_scatter(mix_weight_grad, 'seq', scatter_dimension=0, tiled=True)]
    ppermute x0 -> x44, waiting for transfers between devices: none -> 150 us  [the longest x40 109 us: swap(): return lax.ppermute(array, axis, [(i, i ^ bit) for i in range(count)])]
    all_gather x4 -> x0, waiting for transfers between devices: 143 us -> none  [the longest x2 100 us: entering(): lax.all_gather(a.astype(kind), axis)]
    ppermute x0 -> x44, starting transfers between devices: none -> 52.4 us  [the longest x40 40.1 us: swap(): return lax.ppermute(array, axis, [(i, i ^ bit) for i in range(count)])]
    dot_general x27 -> x30, matrix products: 96.6 us -> 71.1 us  [the longest x6 20.6 us: dot_tn(): lax.dot_general(left, right, (((0,), (0,)), ((), ())), preferred_element_...]
    unnamed x1 -> x0, blocking collectives: 23.5 us -> none
    unnamed x111 -> x180, local copies, waits for them, and re-layouts: 7.72 us -> 25.9 us
    psum x1 -> x0, waiting for transfers between devices: 13 us -> none  [on_device(): lax.psum(summed[0].astype(jnp.bfloat16), 'tp').astype(jnp.float32)]
  transfers between devices with their start and end apart: 12 -> 47, of which waited for: 12 -> 22; matrix products, arithmetic and copies ran while one was open for 10% -> 28% of each run, Pallas kernels for 0% -> 0%
where the time goes in v1:
time: 384 us; the launch traced here: 377 us
  waiting for transfers between devices  150 us (39%)
  matrix products  71.1 us (19%)
  starting transfers between devices  52.9 us (14%)
  local copies, waits for them, and re-layouts  52.6 us (14%)
  other arithmetic  34.4 us (9%)
  between operations  15.4 us (4%)
    ppermute x40, waiting for transfers between devices, swap(): return lax.ppermute(array, axis, [(i, i ^ bit) for i in range(count)])  109 us
    ppermute x4, waiting for transfers between devices, shift(): return lax.ppermute(array, axis, pairs)  40.8 us
    ppermute x40, starting transfers between devices, swap(): return lax.ppermute(array, axis, [(i, i ^ bit) for i in range(count)])  40.1 us
    unnamed x180, local copies, waits for them, and re-layouts  25.9 us
    dot_general x6, matrix products, dot_tn(): lax.dot_general(left, right, (((0,), (0,)), ((), ())), preferred_element_...  20.6 us
    dot_general x5, matrix products, dot_nt(): lax.dot_general(left, right, (((1,), (1,)), ((), ())), preferred_element_...  16.6 us
    ppermute x4, starting transfers between devices, shift(): return lax.ppermute(array, axis, pairs)  12.2 us
    dot_general x12, matrix products, product(): return jnp.einsum(form, left, right, preferred_element_type=F32)  9.22 us
  transfers between devices with their start and end apart: 47, of which 22 were waited for; matrix products, arithmetic and copies ran while one was open for 28% of the time, Pallas kernels for 0%

profile of v1, /device:TPU:0, one launch (start us, length us, event | category | flops | bytes accessed | tf_op | source)
XLA Modules:
  0.0 376.8 jit_solution(12290306020043204273)
XLA Ops:
  10.6 3.1 slice_bitcast_fusion
  13.7 3.6 fusion
  20.1 4.0 %copy.91 = bf16[1024,1024]{1,0:T(8,128)(2,1)} copy(bf16[1024,1024]{0,1:T(8,128)(2,1)} %slice_bitcast_fusion) | data formatting | bytes 4194304 | tf_op jit(solution)/shard_map/dot_general | solution.py:184
  24.8 4.5 %multiply_convert_fusion.11 = (bf16[256,8,128]{0,2,1:T(8,128)(2,1)S(1)}, bf16[256,8,128]{0,2,1:T(8,128)(2,1)S(1)}, bf16[256,8,128]{0,2,1:T(8,128)(2,1)}, bf16[256,8,128]{0,2,1:T(8,128)(2,1)}, f32[256,8,128]{0,2,1:T(8,128)}) fusion(f32[256,128]{0,1:T(8,128)S(1)} %get-tuple-element.89, f32[256,8,128]{0,2,1:T(8,128)} %bitcast.247, ...), kind=kOutput, calls=%fused_computation.121 | convolution fusion | flops 541851648 | bytes 7078912 | tf_op jit(solution)/shard_map/dot_general | solution.py:184
  30.8 3.0 collective-permute-start
  33.8 6.4 %collective-permute-done = bf16[4,256,128]{2,1,0:T(8,128)(2,1)S(1)} collective-permute-done((bf16[4,256,128]{2,1,0:T(8,128)(2,1)}, bf16[4,256,128]{2,1,0:T(8,128)(2,1)S(1)}, u32[]{:S(2)}, u32[]{:S(2)}) %collective-permute-start) | collective-permute-done | bytes 262176 | tf_op jit(solution)/shard_map/ppermute | solution.py:49
  40.5 3.7 collective-permute-start.1
  44.3 4.6 %collective-permute-done.1 = bf16[4,256,128]{2,1,0:T(8,128)(2,1)S(1)} collective-permute-done((bf16[4,256,128]{2,1,0:T(8,128)(2,1)S(1)}, bf16[4,256,128]{2,1,0:T(8,128)(2,1)S(1)}, u32[]{:S(2)}, u32[]{:S(2)}) %collective-permute-start.1) | collective-permute-done | bytes 262176 | tf_op jit(solution)/shard_map/ppermute | solution.py:55
  49.2 5.6 %collective-permute-start.2 = (bf16[4,256,128]{2,1,0:T(8,128)(2,1)S(1)}, bf16[4,256,128]{2,1,0:T(8,128)(2,1)S(1)}, u32[]{:S(2)}, u32[]{:S(2)}) collective-permute-start(bf16[4,256,128]{2,1,0:T(8,128)(2,1)S(1)} %fusion.67), channel_id=1, source_target_pairs={{0,16},{4,20},{8,24},{12,28},{1,17},{5,21},{9,25},{13,29},{2,18},{... | collective-permute-start | bytes 786440 | tf_op jit(solution)/shard_map/ppermute | solution.py:55
  55.7 2.8 collective-permute-done.2
  60.8 4.4 %collective-permute-done.3 = bf16[4,256,128]{2,1,0:T(8,128)(2,1)S(1)} collective-permute-done((bf16[4,256,128]{2,1,0:T(8,128)(2,1)S(1)}, bf16[4,256,128]{2,1,0:T(8,128)(2,1)S(1)}, u32[]{:S(2)}, u32[]{:S(2)}) %collective-permute-start.3) | collective-permute-done | bytes 262176 | tf_op jit(solution)/shard_map/ppermute | solution.py:49
  68.2 3.8 %multiply_convert_fusion.8 = (bf16[256,1024]{1,0:T(8,128)(2,1)S(1)}, f32[256,1024]{1,0:T(8,128)}) fusion(f32[256,1024]{1,0:T(8,128)S(1)} %copy.100, f32[256]{0:T(256)S(1)} %add_rsqrt_fusion.1, bf16[256,1024]{1,0:T(8,128)(2,1)} %fusion.35, bf16[1024,4096]{1,0:T(8,128)(2,1)} %param.13), kind=kOutput, calls=%fused_computation.117 | convolution fusion | flops 537657344 | bytes 5243904 | tf_op jit(solution)/shard_map/dot_general | solution.py:185
  78.4 10.6 %collective-permute-done.5 = bf16[256,1024]{1,0:T(8,128)(2,1)} collective-permute-done((bf16[256,1024]{1,0:T(8,128)(2,1)}, bf16[256,1024]{1,0:T(8,128)(2,1)}, u32[]{:S(2)}, u32[]{:S(2)}) %collective-permute-start.5) | collective-permute-done | bytes 524320 | tf_op jit(solution)/shard_map/ppermute | solution.py:49
  89.5 5.7 %collective-permute-done.10 = bf16[256,1024]{1,0:T(8,128)(2,1)S(1)} collective-permute-done((bf16[256,1024]{1,0:T(8,128)(2,1)S(1)}, bf16[256,1024]{1,0:T(8,128)(2,1)S(1)}, u32[]{:S(2)}, u32[]{:S(2)}) %collective-permute-start.10) | collective-permute-done | bytes 524320 | tf_op jit(solution)/shard_map/ppermute | solution.py:49
  95.2 3.9 %fusion.147 = f32[1024,704]{0,1:T(8,128)S(1)} fusion(bf16[1024,704]{0,1:T(8,128)(2,1)} %param.16, bf16[256,1024]{1,0:T(8,128)(2,1)S(1)} %collective-permute-done.6, bf16[256,1024]{1,0:T(8,128)(2,1)} %collective-permute-done.5, bf16[256,1024]{1,0:T(8,128)(2,1)S(1)} %collective-permute-done.4, bf16[256,1024]{1,0:T(8,128)(2,1)} %multiply_convert_fusion.7), kind=kOutput, calls=%fused_computation.309 | convolution fusion | flops 1484783616 | bytes 6422528 | tf_op jit(solution)/shard_map/dot_general | solution.py:204
  99.2 3.0 fusion.148
  102.2 5.1 %multiply_convert_fusion = (bf16[1024,704]{0,1:T(8,128)(2,1)}, bf16[1024,704]{0,1:T(8,128)(2,1)}, bf16[1024,704]{0,1:T(8,128)(2,1)S(1)}) fusion(f32[1024,704]{0,1:T(8,128)S(1)} %fusion.148, f32[1024,704]{0,1:T(8,128)S(1)} %fusion.147, bf16[1024,704]{0,1:T(8,128)(2,1)S(1)} %copy-done.65, bf16[256,1024]{1,0:T(8,128)(2,1)S(1)} %collective-permute-done.11, ...), kind=kOutput, calls=%fused_computation.3 | convolution fusion | flops 1489108992 | bytes 13631488 | tf_op jit(solution)/shard_map/dot_general | solution.py:191
  108.5 4.1 %convolution_convert_fusion.3 = bf16[1024,704]{0,1:T(8,128)(2,1)} fusion(bf16[1024,704]{0,1:T(8,128)(2,1)S(1)} %get-tuple-element.15, bf16[256,1024]{1,0:T(8,128)(2,1)S(1)} %collective-permute-done.6, bf16[256,1024]{1,0:T(8,128)(2,1)} %collective-permute-done.5, bf16[256,1024]{1,0:T(8,128)(2,1)S(1)} %collective-permute-done.4, ...), kind=kOutput, calls=%fused_computation.38 | convolution fusion | flops 1485504512 | bytes 4980736 | tf_op jit(solution)/shard_map/dot_general | solution.py:31
  112.5 2.5 copy.136
  115.6 4.7 %convolution_convert_fusion.2 = bf16[1024,704]{0,1:T(8,128)(2,1)} fusion(bf16[1024,704]{0,1:T(8,128)(2,1)} %get-tuple-element.13, bf16[256,1024]{1,0:T(8,128)(2,1)} %copy-done.74, bf16[256,1024]{1,0:T(8,128)(2,1)} %collective-permute-done.5, bf16[256,1024]{1,0:T(8,128)(2,1)} %copy-done.73, bf16[256,1024]{1,0:T(8,128)(2,1)} %multiply_convert_fusion.7), kind=kOutput, calls=%fused_computation.37 | convolution fusion | flops 1485504512 | bytes 4980736 | tf_op jit(solution)/shard_map/dot_general | solution.py:31
  120.3 2.6 copy.138
  122.9 3.8 %fusion.162 = f32[1024,1024]{1,0:T(8,128)S(1)} fusion(bf16[1024,704]{0,1:T(8,128)(2,1)} %copy-done.79, bf16[1024,704]{0,1:T(8,128)(2,1)} %param.15), kind=kOutput, calls=%fused_computation.323 | convolution fusion | flops 1476395008 | bytes 7077888 | tf_op jit(solution)/shard_map/dot_general | solution.py:35
  126.7 3.3 add_convert_fusion
  138.2 12.9 %collective-permute-done.19 = bf16[256,1024]{1,0:T(8,128)(2,1)} collective-permute-done((bf16[256,1024]{1,0:T(8,128)(2,1)}, bf16[256,1024]{1,0:T(8,128)(2,1)}, u32[]{:S(2)}, u32[]{:S(2)}) %collective-permute-start.19) | collective-permute-done | bytes 524320 | tf_op jit(solution)/shard_map/ppermute | solution.py:49
  159.1 4.2 %convolution_convert_fusion.1 = bf16[1024,704]{0,1:T(8,128)(2,1)} fusion(bf16[1024,704]{0,1:T(8,128)(2,1)} %get-tuple-element.14, bf16[256,1024]{1,0:T(8,128)(2,1)S(1)} %copy-done.72, bf16[256,1024]{1,0:T(8,128)(2,1)S(1)} %copy-done.68, bf16[256,1024]{1,0:T(8,128)(2,1)S(1)} %copy-done.70, bf16[256,1024]{1,0:T(8,128)(2,1)S(1)} %copy-done.31), kind=kOutput, calls=%fused_computation.36 | convolution fusion | flops 1485504512 | bytes 4980736 | tf_op jit(solution)/shard_map/dot_general | solution.py:31
  163.2 2.6 copy.140
  165.8 11.6 %collective-permute-done.13 = bf16[256,1024]{1,0:T(8,128)(2,1)} collective-permute-done((bf16[256,1024]{1,0:T(8,128)(2,1)}, bf16[256,1024]{1,0:T(8,128)(2,1)}, u32[]{:S(2)}, u32[]{:S(2)}) %collective-permute-start.13) | collective-permute-done | bytes 524320 | tf_op jit(solution)/shard_map/ppermute | solution.py:49
  179.1 9.1 %collective-permute-done.8 = bf16[256,1024]{1,0:T(8,128)(2,1)} collective-permute-done((bf16[256,1024]{1,0:T(8,128)(2,1)}, bf16[256,1024]{1,0:T(8,128)(2,1)}, u32[]{:S(2)}, u32[]{:S(2)}) %collective-permute-start.8) | collective-permute-done | bytes 524320 | tf_op jit(solution)/shard_map/ppermute | solution.py:49
  188.3 3.7 fusion.150
  198.5 6.1 %collective-permute-done.14 = bf16[4,256,128]{2,1,0:T(8,128)(2,1)S(1)} collective-permute-done((bf16[4,256,128]{2,1,0:T(8,128)(2,1)S(1)}, bf16[4,256,128]{2,1,0:T(8,128)(2,1)S(1)}, u32[]{:S(2)}, u32[]{:S(2)}) %collective-permute-start.14) | collective-permute-done | bytes 262176 | tf_op jit(solution)/shard_map/ppermute | solution.py:49
  206.8 21.0 %collective-permute-done.15 = bf16[4,256,128]{2,1,0:T(8,128)(2,1)S(1)} collective-permute-done((bf16[4,256,128]{2,1,0:T(8,128)(2,1)S(1)}, bf16[4,256,128]{2,1,0:T(8,128)(2,1)S(1)}, u32[]{:S(2)}, u32[]{:S(2)}) %collective-permute-start.15) | collective-permute-done | bytes 262176 | tf_op jit(solution)/shard_map/ppermute | solution.py:55
  230.9 12.5 %collective-permute-done.16 = bf16[4,256,128]{2,1,0:T(8,128)(2,1)S(1)} collective-permute-done((bf16[4,256,128]{2,1,0:T(8,128)(2,1)S(1)}, bf16[4,256,128]{2,1,0:T(8,128)(2,1)S(1)}, u32[]{:S(2)}, u32[]{:S(2)}) %collective-permute-start.16) | collective-permute-done | bytes 262176 | tf_op jit(solution)/shard_map/ppermute | solution.py:55
  247.3 6.9 %collective-permute-done.17 = bf16[4,256,128]{2,1,0:T(8,128)(2,1)S(1)} collective-permute-done((bf16[4,256,128]{2,1,0:T(8,128)(2,1)S(1)}, bf16[4,256,128]{2,1,0:T(8,128)(2,1)S(1)}, u32[]{:S(2)}, u32[]{:S(2)}) %collective-permute-start.17) | collective-permute-done | bytes 262176 | tf_op jit(solution)/shard_map/ppermute | solution.py:49
  267.7 4.1 %collective-permute-done.35 = bf16[256,512]{1,0:T(8,128)(2,1)} collective-permute-done((bf16[256,512]{1,0:T(8,128)(2,1)}, bf16[256,512]{1,0:T(8,128)(2,1)}, u32[]{:S(2)}, u32[]{:S(2)}) %collective-permute-start.35) | collective-permute-done | bytes 262176 | tf_op jit(solution)/shard_map/ppermute | solution.py:49
  273.3 3.2 collective-permute-done.36
  278.6 3.0 convolution_convert_fusion.4
  285.8 7.5 %collective-permute-done.23 = bf16[256,768]{1,0:T(8,128)(2,1)S(1)} collective-permute-done((bf16[256,768]{1,0:T(8,128)(2,1)S(1)}, bf16[256,768]{1,0:T(8,128)(2,1)S(1)}, u32[]{:S(2)}, u32[]{:S(2)}) %collective-permute-start.23) | collective-permute-done | bytes 393248 | tf_op jit(solution)/shard_map/ppermute | solution.py:49
  293.4 2.8 convolution_convert_fusion.5
  299.3 3.0 reshape.369
  302.4 4.9 %constant_dynamic-slice_fusion.1 = (bf16[4,1,128,768]{2,1,0,3:T(2,128)(2,1)}, bf16[4,1,128,768]{2,1,0,3:T(2,128)(2,1)}) fusion(bf16[4,2,128,768]{2,1,0,3:T(2,128)(2,1)S(1)} %reshape.369, s32[]{:T(128)S(6)} %select_n.308, s32[]{:T(128)S(6)} %select_n.309), kind=kLoop, calls=%fused_computation.277 | loop fusion | bytes 3145736 | tf_op jit(solution)/shard_map/jit(dynamic_index_in_dim)/dynamic_slice | solution.py:93
  307.3 4.7 %copy.144 = bf16[4,1,128,768]{3,2,0,1:T(8,128)(2,1)} copy(bf16[4,1,128,768]{2,1,0,3:T(2,128)(2,1)} %get-tuple-element.25) | data formatting | bytes 1572864
  316.8 4.4 %collective-permute-start.40 = (bf16[128,512]{1,0:T(8,128)(2,1)S(1)}, bf16[128,512]{1,0:T(8,128)(2,1)}, u32[]{:S(2)}, u32[]{:S(2)}) collective-permute-start(bf16[128,512]{1,0:T(8,128)(2,1)S(1)} %get-tuple-element.55), channel_id=1, source_target_pairs={{0,24},{4,28},{8,16},{12,20},{16,8},{20,12},{24,0},{28,4},{1,25},{... | collective-permute-start | bytes 393224 | tf_op jit(solution)/shard_map/ppermute | solution.py:49
  321.2 6.7 %fusion.36 = (f32[256]{0:T(256)S(1)}, f32[256,1024]{1,0:T(8,128)}) fusion(bf16[1,256,1024]{2,1,0:T(8,128)(2,1)S(1)} %copy-done.7, bf16[1024,4096]{1,0:T(8,128)(2,1)} %param.13, bf16[256,1024]{1,0:T(8,128)(2,1)S(1)} %copy-done.24, bf16[256,1024]{1,0:T(8,128)(2,1)S(1)} %copy.135, bf16[256,1024]{1,0:T(8,128)(2,1)S(1)} %copy.116, ...), kind=kOutput, calls=%fused_computation.66 | convolution fusion | flops 2156658432 | bytes 12059648 | tf_op jit(solution)/shard_map/dot_general | solution.py:35
  329.3 4.6 %collective-permute-done.39 = bf16[128,512]{1,0:T(8,128)(2,1)S(1)} collective-permute-done((bf16[128,512]{1,0:T(8,128)(2,1)}, bf16[128,512]{1,0:T(8,128)(2,1)S(1)}, u32[]{:S(2)}, u32[]{:S(2)}) %collective-permute-start.39) | collective-permute-done | bytes 131104 | tf_op jit(solution)/shard_map/ppermute | solution.py:49
  337.8 3.9 %collective-permute-start.28 = (bf16[128,768]{1,0:T(8,128)(2,1)S(1)}, bf16[128,768]{1,0:T(8,128)(2,1)S(1)}, u32[]{:S(2)}, u32[]{:S(2)}) collective-permute-start(bf16[128,768]{1,0:T(8,128)(2,1)S(1)} %get-tuple-element.43), channel_id=1, source_target_pairs={{0,8},{4,12},{8,0},{12,4},{16,24},{20,28},{24,16},{28,20},{1,9},{5... | collective-permute-start | bytes 589832 | tf_op jit(solution)/shard_map/ppermute | solution.py:49
  341.7 2.4 collective-permute-start.30
  344.7 3.9 %collective-permute-done.28 = bf16[128,768]{1,0:T(8,128)(2,1)S(1)} collective-permute-done((bf16[128,768]{1,0:T(8,128)(2,1)S(1)}, bf16[128,768]{1,0:T(8,128)(2,1)S(1)}, u32[]{:S(2)}, u32[]{:S(2)}) %collective-permute-start.28) | collective-permute-done | bytes 196640 | tf_op jit(solution)/shard_map/ppermute | solution.py:49
  348.6 9.7 %collective-permute-done.29 = bf16[128,768]{1,0:T(8,128)(2,1)S(1)} collective-permute-done((bf16[128,768]{1,0:T(8,128)(2,1)S(1)}, bf16[128,768]{1,0:T(8,128)(2,1)S(1)}, u32[]{:S(2)}, u32[]{:S(2)}) %collective-permute-start.29) | collective-permute-done | bytes 196640 | tf_op jit(solution)/shard_map/ppermute | solution.py:49
  (347 shorter events, 103.1 us)
Async XLA Ops:
  7.2 64.9 %copy-start = (bf16[1024,1024]{1,0:T(8,128)(2,1)S(1)}, bf16[1024,1024]{1,0:T(8,128)(2,1)}, u32[]{:S(2)}) copy-start(bf16[1024,1024]{1,0:T(8,128)(2,1)} %param.14) | copy-start | bytes 6291460
  7.2 352.8 %reduce-scatter.10.cloned.1.call-start = ((), (), s32[]{:S(2)}) async-start(), calls=%async_computation.3 | async-start | bytes 1769472
  30.8 9.5 %collective-permute-start = (bf16[4,256,128]{2,1,0:T(8,128)(2,1)}, bf16[4,256,128]{2,1,0:T(8,128)(2,1)S(1)}, u32[]{:S(2)}, u32[]{:S(2)}) collective-permute-start(bf16[4,256,128]{2,1,0:T(8,128)(2,1)} %constant_dynamic-slice_fusion.3), channel_id=1, source_target_pairs={{0,4},{4,0},{8,12},{12,8},{16,20},{20,16},{24,28},{28,24},{1,5},{5... | collective-permute-start | bytes 786440 | tf_op jit(solution)/shard_map/ppermute | solution.py:49
  40.5 8.4 %collective-permute-start.1 = (bf16[4,256,128]{2,1,0:T(8,128)(2,1)S(1)}, bf16[4,256,128]{2,1,0:T(8,128)(2,1)S(1)}, u32[]{:S(2)}, u32[]{:S(2)}) collective-permute-start(bf16[4,256,128]{2,1,0:T(8,128)(2,1)S(1)} %fusion.109), channel_id=1, source_target_pairs={{0,8},{4,12},{8,16},{12,20},{16,24},{20,28},{1,9},{5,13},{9,17},{1... | collective-permute-start | bytes 786440 | tf_op jit(solution)/shard_map/ppermute | solution.py:55
  49.2 9.3 %collective-permute-start.2 = (bf16[4,256,128]{2,1,0:T(8,128)(2,1)S(1)}, bf16[4,256,128]{2,1,0:T(8,128)(2,1)S(1)}, u32[]{:S(2)}, u32[]{:S(2)}) collective-permute-start(bf16[4,256,128]{2,1,0:T(8,128)(2,1)S(1)} %fusion.67), channel_id=1, source_target_pairs={{0,16},{4,20},{8,24},{12,28},{1,17},{5,21},{9,25},{13,29},{2,18},{... | collective-permute-start | bytes 786440 | tf_op jit(solution)/shard_map/ppermute | solution.py:55
  58.8 6.4 %collective-permute-start.3 = (bf16[4,256,128]{2,1,0:T(8,128)(2,1)S(1)}, bf16[4,256,128]{2,1,0:T(8,128)(2,1)S(1)}, u32[]{:S(2)}, u32[]{:S(2)}) collective-permute-start(bf16[4,256,128]{2,1,0:T(8,128)(2,1)S(1)} %get-tuple-element.49), channel_id=1, source_target_pairs={{0,4},{4,0},{8,12},{12,8},{16,20},{20,16},{24,28},{28,24},{1,5},{5... | collective-permute-start | bytes 786440 | tf_op jit(solution)/shard_map/ppermute | solution.py:49
  73.8 15.2 %collective-permute-start.5 = (bf16[256,1024]{1,0:T(8,128)(2,1)}, bf16[256,1024]{1,0:T(8,128)(2,1)}, u32[]{:S(2)}, u32[]{:S(2)}) collective-permute-start(bf16[256,1024]{1,0:T(8,128)(2,1)} %multiply_convert_fusion.7), channel_id=1, source_target_pairs={{0,2},{1,3},{2,0},{3,1},{4,6},{5,7},{6,4},{7,5},{8,10},{9,11},{10,... | collective-permute-start | bytes 1572872 | tf_op jit(solution)/shard_map/ppermute | solution.py:49
  77.8 17.4 %collective-permute-start.10 = (bf16[256,1024]{1,0:T(8,128)(2,1)S(1)}, bf16[256,1024]{1,0:T(8,128)(2,1)S(1)}, u32[]{:S(2)}, u32[]{:S(2)}) collective-permute-start(bf16[256,1024]{1,0:T(8,128)(2,1)S(1)} %fusion.58), channel_id=1, source_target_pairs={{0,2},{1,3},{2,0},{3,1},{4,6},{5,7},{6,4},{7,5},{8,10},{9,11},{10,... | collective-permute-start | bytes 1572872 | tf_op jit(solution)/shard_map/ppermute | solution.py:49
  78.4 16.8 %collective-permute-start.4 = (bf16[256,1024]{1,0:T(8,128)(2,1)}, bf16[256,1024]{1,0:T(8,128)(2,1)S(1)}, u32[]{:S(2)}, u32[]{:S(2)}) collective-permute-start(bf16[256,1024]{1,0:T(8,128)(2,1)} %multiply_convert_fusion.7), channel_id=1, source_target_pairs={{0,1},{1,0},{2,3},{3,2},{4,5},{5,4},{6,7},{7,6},{8,9},{9,8},{10,11... | collective-permute-start | bytes 1572872 | tf_op jit(solution)/shard_map/ppermute | solution.py:49
  89.0 6.2 %collective-permute-start.6 = (bf16[256,1024]{1,0:T(8,128)(2,1)}, bf16[256,1024]{1,0:T(8,128)(2,1)S(1)}, u32[]{:S(2)}, u32[]{:S(2)}) collective-permute-start(bf16[256,1024]{1,0:T(8,128)(2,1)} %collective-permute-done.5), channel_id=1, source_target_pairs={{0,1},{1,0},{2,3},{3,2},{4,5},{5,4},{6,7},{7,6},{8,9},{9,8},{10,11... | collective-permute-start | bytes 1572872 | tf_op jit(solution)/shard_map/ppermute | solution.py:49
  89.0 13.2 %collective-permute-start.9 = (bf16[256,1024]{1,0:T(8,128)(2,1)S(1)}, bf16[256,1024]{1,0:T(8,128)(2,1)S(1)}, u32[]{:S(2)}, u32[]{:S(2)}) collective-permute-start(bf16[256,1024]{1,0:T(8,128)(2,1)S(1)} %fusion.58), channel_id=1, source_target_pairs={{0,1},{1,0},{2,3},{3,2},{4,5},{5,4},{6,7},{7,6},{8,9},{9,8},{10,11... | collective-permute-start | bytes 1572872 | tf_op jit(solution)/shard_map/ppermute | solution.py:49
  95.2 7.0 %collective-permute-start.11 = (bf16[256,1024]{1,0:T(8,128)(2,1)S(1)}, bf16[256,1024]{1,0:T(8,128)(2,1)S(1)}, u32[]{:S(2)}, u32[]{:S(2)}) collective-permute-start(bf16[256,1024]{1,0:T(8,128)(2,1)S(1)} %collective-permute-done.10), channel_id=1, source_target_pairs={{0,1},{1,0},{2,3},{3,2},{4,5},{5,4},{6,7},{7,6},{8,9},{9,8},{10,11... | collective-permute-start | bytes 1572872 | tf_op jit(solution)/shard_map/ppermute | solution.py:49
  115.1 246.8 %reduce-scatter.12.cloned.1.call-start = ((), (), s32[]{:S(2)}) async-start(), calls=%async_computation.4 | async-start | bytes 1769472
  130.0 233.7 %reduce-scatter.14.cloned.1.call-start = ((), (), s32[]{:S(2)}) async-start(), calls=%async_computation.5 | async-start | bytes 1769472
  132.6 20.0 %collective-permute-start.12 = (bf16[2,256,1024]{2,1,0:T(8,128)(2,1)}, bf16[2,256,1024]{2,1,0:T(8,128)(2,1)}, u32[]{:S(2)}, u32[]{:S(2)}) collective-permute-start(bf16[2,256,1024]{2,1,0:T(8,128)(2,1)} %pad_maximum_fusion.9), channel_id=1, source_target_pairs={{0,1},{1,0},{2,3},{3,2},{4,5},{5,4},{6,7},{7,6},{8,9},{9,8},{10,11... | collective-permute-start | bytes 3145736 | tf_op jit(solution)/shard_map/ppermute | solution.py:49
  136.5 18.9 %collective-permute-start.7 = (bf16[2,256,1024]{2,1,0:T(8,128)(2,1)}, bf16[2,256,1024]{2,1,0:T(8,128)(2,1)}, u32[]{:S(2)}, u32[]{:S(2)}) collective-permute-start(bf16[2,256,1024]{2,1,0:T(8,128)(2,1)} %pad_maximum_fusion.8), channel_id=1, source_target_pairs={{0,1},{1,0},{2,3},{3,2},{4,5},{5,4},{6,7},{7,6},{8,9},{9,8},{10,11... | collective-permute-start | bytes 3145736 | tf_op jit(solution)/shard_map/ppermute | solution.py:49
  136.7 14.5 %collective-permute-start.19 = (bf16[256,1024]{1,0:T(8,128)(2,1)}, bf16[256,1024]{1,0:T(8,128)(2,1)}, u32[]{:S(2)}, u32[]{:S(2)}) collective-permute-start(bf16[256,1024]{1,0:T(8,128)(2,1)} %fusion.35), channel_id=1, source_target_pairs={{0,2},{1,3},{2,0},{3,1},{4,6},{5,7},{6,4},{7,5},{8,10},{9,11},{10,... | collective-permute-start | bytes 1572872 | tf_op jit(solution)/shard_map/ppermute | solution.py:49
  138.1 126.7 %collective-permute-start.18 = (bf16[256,1024]{1,0:T(8,128)(2,1)}, bf16[256,1024]{1,0:T(8,128)(2,1)}, u32[]{:S(2)}, u32[]{:S(2)}) collective-permute-start(bf16[256,1024]{1,0:T(8,128)(2,1)} %fusion.35), channel_id=1, source_target_pairs={{0,1},{1,0},{2,3},{3,2},{4,5},{5,4},{6,7},{7,6},{8,9},{9,8},{10,11... | collective-permute-start | bytes 1572872 | tf_op jit(solution)/shard_map/ppermute | solution.py:49
  151.2 114.8 %collective-permute-start.20 = (bf16[256,1024]{1,0:T(8,128)(2,1)}, bf16[256,1024]{1,0:T(8,128)(2,1)}, u32[]{:S(2)}, u32[]{:S(2)}) collective-permute-start(bf16[256,1024]{1,0:T(8,128)(2,1)} %collective-permute-done.19), channel_id=1, source_target_pairs={{0,1},{1,0},{2,3},{3,2},{4,5},{5,4},{6,7},{7,6},{8,9},{9,8},{10,11... | collective-permute-start | bytes 1572872 | tf_op jit(solution)/shard_map/ppermute | solution.py:49
  151.2 116.0 %collective-permute-start.25 = (bf16[256,1024]{1,0:T(8,128)(2,1)}, bf16[256,1024]{1,0:T(8,128)(2,1)}, u32[]{:S(2)}, u32[]{:S(2)}) collective-permute-start(bf16[256,1024]{1,0:T(8,128)(2,1)} %copy-done.21), channel_id=1, source_target_pairs={{0,2},{1,3},{2,0},{3,1},{4,6},{5,7},{6,4},{7,5},{8,10},{9,11},{10,... | collective-permute-start | bytes 1572872 | tf_op jit(solution)/shard_map/ppermute | solution.py:49
  154.8 22.6 %collective-permute-start.13 = (bf16[256,1024]{1,0:T(8,128)(2,1)}, bf16[256,1024]{1,0:T(8,128)(2,1)}, u32[]{:S(2)}, u32[]{:S(2)}) collective-permute-start(bf16[256,1024]{1,0:T(8,128)(2,1)} %fusion.55), channel_id=1, source_target_pairs={{0,2},{1,3},{2,0},{3,1},{4,6},{5,7},{6,4},{7,5},{8,10},{9,11},{10,... | collective-permute-start | bytes 1572872 | tf_op jit(solution)/shard_map/ppermute | solution.py:49
  157.6 30.7 %collective-permute-start.8 = (bf16[256,1024]{1,0:T(8,128)(2,1)}, bf16[256,1024]{1,0:T(8,128)(2,1)}, u32[]{:S(2)}, u32[]{:S(2)}) collective-permute-start(bf16[256,1024]{1,0:T(8,128)(2,1)} %fusion.59), channel_id=1, source_target_pairs={{0,2},{1,3},{2,0},{3,1},{4,6},{5,7},{6,4},{7,5},{8,10},{9,11},{10,... | collective-permute-start | bytes 1572872 | tf_op jit(solution)/shard_map/ppermute | solution.py:49
  196.0 8.7 %collective-permute-start.14 = (bf16[4,256,128]{2,1,0:T(8,128)(2,1)S(1)}, bf16[4,256,128]{2,1,0:T(8,128)(2,1)S(1)}, u32[]{:S(2)}, u32[]{:S(2)}) collective-permute-start(bf16[4,256,128]{2,1,0:T(8,128)(2,1)S(1)} %constant_dynamic-slice_fusion.2), channel_id=1, source_target_pairs={{0,4},{4,0},{8,12},{12,8},{16,20},{20,16},{24,28},{28,24},{1,5},{5... | collective-permute-start | bytes 786440 | tf_op jit(solution)/shard_map/ppermute | solution.py:49
  204.9 22.9 %collective-permute-start.15 = (bf16[4,256,128]{2,1,0:T(8,128)(2,1)S(1)}, bf16[4,256,128]{2,1,0:T(8,128)(2,1)S(1)}, u32[]{:S(2)}, u32[]{:S(2)}) collective-permute-start(bf16[4,256,128]{2,1,0:T(8,128)(2,1)S(1)} %fusion.108), channel_id=1, source_target_pairs={{8,0},{12,4},{16,8},{20,12},{24,16},{28,20},{9,1},{13,5},{17,9},{2... | collective-permute-start | bytes 786440 | tf_op jit(solution)/shard_map/ppermute | solution.py:55
  228.1 15.3 %collective-permute-start.16 = (bf16[4,256,128]{2,1,0:T(8,128)(2,1)S(1)}, bf16[4,256,128]{2,1,0:T(8,128)(2,1)S(1)}, u32[]{:S(2)}, u32[]{:S(2)}) collective-permute-start(bf16[4,256,128]{2,1,0:T(8,128)(2,1)S(1)} %fusion.69), channel_id=1, source_target_pairs={{16,0},{20,4},{24,8},{28,12},{17,1},{21,5},{25,9},{29,13},{18,2},{... | collective-permute-start | bytes 786440 | tf_op jit(solution)/shard_map/ppermute | solution.py:55
  243.7 10.6 %collective-permute-start.17 = (bf16[4,256,128]{2,1,0:T(8,128)(2,1)S(1)}, bf16[4,256,128]{2,1,0:T(8,128)(2,1)S(1)}, u32[]{:S(2)}, u32[]{:S(2)}) collective-permute-start(bf16[4,256,128]{2,1,0:T(8,128)(2,1)S(1)} %get-tuple-element.47), channel_id=1, source_target_pairs={{0,4},{4,0},{8,12},{12,8},{16,20},{20,16},{24,28},{28,24},{1,5},{5... | collective-permute-start | bytes 786440 | tf_op jit(solution)/shard_map/ppermute | solution.py:49
  262.3 5.1 %collective-permute-start.34 = (bf16[256,512]{1,0:T(8,128)(2,1)}, bf16[256,512]{1,0:T(8,128)(2,1)}, u32[]{:S(2)}, u32[]{:S(2)}) collective-permute-start(bf16[256,512]{1,0:T(8,128)(2,1)} %get-tuple-element.34), channel_id=1, source_target_pairs={{0,1},{1,0},{2,3},{3,2},{4,5},{5,4},{6,7},{7,6},{8,9},{9,8},{10,11... | collective-permute-start | bytes 786440 | tf_op jit(solution)/shard_map/ppermute | solution.py:49
  262.3 9.5 %collective-permute-start.35 = (bf16[256,512]{1,0:T(8,128)(2,1)}, bf16[256,512]{1,0:T(8,128)(2,1)}, u32[]{:S(2)}, u32[]{:S(2)}) collective-permute-start(bf16[256,512]{1,0:T(8,128)(2,1)} %get-tuple-element.33), channel_id=1, source_target_pairs={{0,2},{1,3},{2,0},{3,1},{4,6},{5,7},{6,4},{7,5},{8,10},{9,11},{10,... | collective-permute-start | bytes 786440 | tf_op jit(solution)/shard_map/ppermute | solution.py:49
  265.2 11.2 %collective-permute-start.36 = (bf16[256,512]{1,0:T(8,128)(2,1)S(1)}, bf16[256,512]{1,0:T(8,128)(2,1)S(1)}, u32[]{:S(2)}, u32[]{:S(2)}) collective-permute-start(bf16[256,512]{1,0:T(8,128)(2,1)S(1)} %copy-done.55), channel_id=1, source_target_pairs={{0,3},{1,2},{2,1},{3,0},{4,7},{5,6},{6,5},{7,4},{8,11},{9,10},{10,... | collective-permute-start | bytes 786440 | tf_op jit(solution)/shard_map/ppermute | solution.py:49
  266.8 29.4 %collective-permute-start.24 = (bf16[256,1024]{1,0:T(8,128)(2,1)S(1)}, bf16[256,1024]{1,0:T(8,128)(2,1)S(1)}, u32[]{:S(2)}, u32[]{:S(2)}) collective-permute-start(bf16[256,1024]{1,0:T(8,128)(2,1)S(1)} %copy-done.22), channel_id=1, source_target_pairs={{0,1},{1,0},{2,3},{3,2},{4,5},{5,4},{6,7},{7,6},{8,9},{9,8},{10,11... | collective-permute-start | bytes 1572872 | tf_op jit(solution)/shard_map/ppermute | solution.py:49
  267.2 29.1 %collective-permute-start.26 = (bf16[256,1024]{1,0:T(8,128)(2,1)}, bf16[256,1024]{1,0:T(8,128)(2,1)S(1)}, u32[]{:S(2)}, u32[]{:S(2)}) collective-permute-start(bf16[256,1024]{1,0:T(8,128)(2,1)} %collective-permute-done.25), channel_id=1, source_target_pairs={{0,1},{1,0},{2,3},{3,2},{4,5},{5,4},{6,7},{7,6},{8,9},{9,8},{10,11... | collective-permute-start | bytes 1572872 | tf_op jit(solution)/shard_map/ppermute | solution.py:49
  267.3 15.2 %collective-permute-start.21 = (bf16[256,768]{1,0:T(8,128)(2,1)S(1)}, bf16[256,768]{1,0:T(8,128)(2,1)S(1)}, u32[]{:S(2)}, u32[]{:S(2)}) collective-permute-start(bf16[256,768]{1,0:T(8,128)(2,1)S(1)} %get-tuple-element.29), channel_id=1, source_target_pairs={{0,1},{1,0},{2,3},{3,2},{4,5},{5,4},{6,7},{7,6},{8,9},{9,8},{10,11... | collective-permute-start | bytes 1179656 | tf_op jit(solution)/shard_map/ppermute | solution.py:49
  271.8 13.9 %collective-permute-start.22 = (bf16[256,768]{1,0:T(8,128)(2,1)S(1)}, bf16[256,768]{1,0:T(8,128)(2,1)S(1)}, u32[]{:S(2)}, u32[]{:S(2)}) collective-permute-start(bf16[256,768]{1,0:T(8,128)(2,1)S(1)} %get-tuple-element.28), channel_id=1, source_target_pairs={{0,2},{1,3},{2,0},{3,1},{4,6},{5,7},{6,4},{7,5},{8,10},{9,11},{10,... | collective-permute-start | bytes 1179656 | tf_op jit(solution)/shard_map/ppermute | solution.py:49
  276.4 16.9 %collective-permute-start.23 = (bf16[256,768]{1,0:T(8,128)(2,1)S(1)}, bf16[256,768]{1,0:T(8,128)(2,1)S(1)}, u32[]{:S(2)}, u32[]{:S(2)}) collective-permute-start(bf16[256,768]{1,0:T(8,128)(2,1)S(1)} %get-tuple-element.27), channel_id=1, source_target_pairs={{0,3},{1,2},{2,1},{3,0},{4,7},{5,6},{6,5},{7,4},{8,11},{9,10},{10,... | collective-permute-start | bytes 1179656 | tf_op jit(solution)/shard_map/ppermute | solution.py:49
  282.5 31.3 %collective-permute-start.37 = (bf16[4,128,512]{2,1,0:T(8,128)(2,1)}, bf16[4,128,512]{2,1,0:T(8,128)(2,1)}, u32[]{:S(2)}, u32[]{:S(2)}) collective-permute-start(bf16[4,128,512]{2,1,0:T(8,128)(2,1)} %dynamic-slice_bitcast_fusion), channel_id=1, source_target_pairs={{0,4},{4,0},{8,12},{12,8},{16,20},{20,16},{24,28},{28,24},{1,5},{5... | collective-permute-start | bytes 1572872 | tf_op jit(solution)/shard_map/ppermute | solution.py:49
  312.0 24.4 %collective-permute-start.27 = (bf16[4,128,768]{2,1,0:T(8,128)(2,1)}, bf16[4,128,768]{2,1,0:T(8,128)(2,1)}, u32[]{:S(2)}, u32[]{:S(2)}) collective-permute-start(bf16[4,128,768]{2,1,0:T(8,128)(2,1)} %bitcast.255), channel_id=1, source_target_pairs={{0,4},{4,0},{8,12},{12,8},{16,20},{20,16},{24,28},{28,24},{1,5},{5... | collective-permute-start | bytes 2359304 | tf_op jit(solution)/shard_map/ppermute | solution.py:49
  316.8 12.5 %collective-permute-start.38 = (bf16[128,512]{1,0:T(8,128)(2,1)}, bf16[128,512]{1,0:T(8,128)(2,1)S(1)}, u32[]{:S(2)}, u32[]{:S(2)}) collective-permute-start(bf16[128,512]{1,0:T(8,128)(2,1)} %get-tuple-element.54), channel_id=1, source_target_pairs={{0,8},{4,12},{8,0},{12,4},{16,24},{20,28},{24,16},{28,20},{1,9},{5... | collective-permute-start | bytes 393224 | tf_op jit(solution)/shard_map/ppermute | solution.py:49
  316.8 17.1 %collective-permute-start.39 = (bf16[128,512]{1,0:T(8,128)(2,1)}, bf16[128,512]{1,0:T(8,128)(2,1)S(1)}, u32[]{:S(2)}, u32[]{:S(2)}) collective-permute-start(bf16[128,512]{1,0:T(8,128)(2,1)} %get-tuple-element.56), channel_id=1, source_target_pairs={{0,16},{4,20},{8,24},{12,28},{16,0},{20,4},{24,8},{28,12},{1,17},{... | collective-permute-start | bytes 393224 | tf_op jit(solution)/shard_map/ppermute | solution.py:49
  316.8 17.1 %collective-permute-start.40 = (bf16[128,512]{1,0:T(8,128)(2,1)S(1)}, bf16[128,512]{1,0:T(8,128)(2,1)}, u32[]{:S(2)}, u32[]{:S(2)}) collective-permute-start(bf16[128,512]{1,0:T(8,128)(2,1)S(1)} %get-tuple-element.55), channel_id=1, source_target_pairs={{0,24},{4,28},{8,16},{12,20},{16,8},{20,12},{24,0},{28,4},{1,25},{... | collective-permute-start | bytes 393224 | tf_op jit(solution)/shard_map/ppermute | solution.py:49
  335.1 9.1 %collective-permute-start.42 = (bf16[128,512]{1,0:T(8,128)(2,1)S(1)}, bf16[128,512]{1,0:T(8,128)(2,1)S(1)}, u32[]{:S(2)}, u32[]{:S(2)}) collective-permute-start(bf16[128,512]{1,0:T(8,128)(2,1)S(1)} %fusion.121), channel_id=1, source_target_pairs={{0,2},{1,3},{2,0},{3,1},{4,6},{5,7},{6,4},{7,5},{8,10},{9,11},{10,... | collective-permute-start | bytes 393224 | tf_op jit(solution)/shard_map/ppermute | solution.py:49
  337.8 10.7 %collective-permute-start.28 = (bf16[128,768]{1,0:T(8,128)(2,1)S(1)}, bf16[128,768]{1,0:T(8,128)(2,1)S(1)}, u32[]{:S(2)}, u32[]{:S(2)}) collective-permute-start(bf16[128,768]{1,0:T(8,128)(2,1)S(1)} %get-tuple-element.43), channel_id=1, source_target_pairs={{0,8},{4,12},{8,0},{12,4},{16,24},{20,28},{24,16},{28,20},{1,9},{5... | collective-permute-start | bytes 589832 | tf_op jit(solution)/shard_map/ppermute | solution.py:49
  341.7 16.5 %collective-permute-start.29 = (bf16[128,768]{1,0:T(8,128)(2,1)S(1)}, bf16[128,768]{1,0:T(8,128)(2,1)S(1)}, u32[]{:S(2)}, u32[]{:S(2)}) collective-permute-start(bf16[128,768]{1,0:T(8,128)(2,1)S(1)} %get-tuple-element.45), channel_id=1, source_target_pairs={{0,16},{4,20},{8,24},{12,28},{16,0},{20,4},{24,8},{28,12},{1,17},{... | collective-permute-start | bytes 589832 | tf_op jit(solution)/shard_map/ppermute | solution.py:49
  341.7 16.5 %collective-permute-start.30 = (bf16[128,768]{1,0:T(8,128)(2,1)S(1)}, bf16[128,768]{1,0:T(8,128)(2,1)S(1)}, u32[]{:S(2)}, u32[]{:S(2)}) collective-permute-start(bf16[128,768]{1,0:T(8,128)(2,1)S(1)} %get-tuple-element.44), channel_id=1, source_target_pairs={{0,24},{4,28},{8,16},{12,20},{16,8},{20,12},{24,0},{28,4},{1,25},{... | collective-permute-start | bytes 589832 | tf_op jit(solution)/shard_map/ppermute | solution.py:49
  344.2 21.9 %collective-permute-start.41 = (bf16[128,512]{1,0:T(8,128)(2,1)S(1)}, bf16[128,512]{1,0:T(8,128)(2,1)S(1)}, u32[]{:S(2)}, u32[]{:S(2)}) collective-permute-start(bf16[128,512]{1,0:T(8,128)(2,1)S(1)} %fusion.121), channel_id=1, source_target_pairs={{0,1},{1,0},{2,3},{3,2},{4,5},{5,4},{6,7},{7,6},{8,9},{9,8},{10,11... | collective-permute-start | bytes 393224 | tf_op jit(solution)/shard_map/ppermute | solution.py:49
  344.2 21.9 %collective-permute-start.43 = (bf16[128,512]{1,0:T(8,128)(2,1)S(1)}, bf16[128,512]{1,0:T(8,128)(2,1)S(1)}, u32[]{:S(2)}, u32[]{:S(2)}) collective-permute-start(bf16[128,512]{1,0:T(8,128)(2,1)S(1)} %collective-permute-done.42), channel_id=1, source_target_pairs={{0,1},{1,0},{2,3},{3,2},{4,5},{5,4},{6,7},{7,6},{8,9},{9,8},{10,11... | collective-permute-start | bytes 393224 | tf_op jit(solution)/shard_map/ppermute | solution.py:49
  358.3 7.3 %collective-permute-start.32 = (bf16[128,768]{1,0:T(8,128)(2,1)S(1)}, bf16[128,768]{1,0:T(8,128)(2,1)S(1)}, u32[]{:S(2)}, u32[]{:S(2)}) collective-permute-start(bf16[128,768]{1,0:T(8,128)(2,1)S(1)} %fusion.107), channel_id=1, source_target_pairs={{0,2},{1,3},{2,0},{3,1},{4,6},{5,7},{6,4},{7,5},{8,10},{9,11},{10,... | collective-permute-start | bytes 589832 | tf_op jit(solution)/shard_map/ppermute | solution.py:49
  365.6 1.4 collective-permute-start.31
  365.6 1.7 collective-permute-start.33
  (79 other events, 624.8 us)
Sparse Core Ops, SparseCore 0:
  115.2 77.1 reduce-scatter.9
  196.2 64.7 reduce-scatter.11
  264.4 71.4 reduce-scatter.13
